TPU v7x, 32 devices: a whole 2x2x4 slice. The times are simulated.
32 devices in a mesh: var: 8 (over y, x, core), smp: 4 (over z).
Axes of the slice: x: 2, y: 2, z: 4, core: 2. Of those that a mesh axis runs over, the one named last changes fastest.
Arguments:
- dosage: bfloat16 [4096, 4096], P('smp', 'var'), may hold values from -6 to 6
- trait_class: int32 [4096], P('smp'), may hold values from 0 to 15
- class_effect: float32 [16], replicated, may hold values from -4 to 4
Outputs:
- interaction: float32 [4096, 1536], P(('var', 'smp'))
All inputs are finite; a program needn't handle non-finite values.
Results may differ from a plain program's by a relative error of at most 0.0029.
Values may be sent and summed in bfloat16 or wider, within the bound.
A program may use at most 64 MiB of HBM per device.

v0:
```python
import jax
import jax.numpy as jnp
from jax import lax
from jax.sharding import PartitionSpec as P


def from_behind(value, axis, steps):
    count = lax.axis_size(axis)
    pairs = [(source, (source + steps) % count) for source in range(count)]
    return lax.ppermute(value, axis, pairs)


def shards(dosage, trait_class, class_effect):
    classes = class_effect.shape[0]
    centred = class_effect - jnp.mean(class_effect)
    picks = trait_class[:, None] == jnp.arange(classes, dtype=jnp.int32)[None, :]
    trait = jnp.sum(jnp.where(picks, centred[None, :], jnp.float32(0.0)), axis=1)
    values = dosage.astype(jnp.float32)
    weighted = (trait[:, None] * values).astype(jnp.bfloat16)
    squared = (values * values).astype(jnp.bfloat16)
    contract = (((0,), (0,)), ((), ()))
    before = from_behind(dosage, "var", 1)
    after = from_behind(before, "var", -2)
    right = jnp.concatenate([before, dosage, after], axis=1)
    right_values = right.astype(jnp.float32)
    right_sq = (right_values * right_values).astype(jnp.bfloat16)
    cross = lax.dot_general(weighted, right, contract, preferred_element_type=jnp.float32)
    fourth = lax.dot_general(squared, right_sq, contract, preferred_element_type=jnp.float32)
    cross, fourth = (
        lax.psum_scatter(cross, "smp", scatter_dimension=0, tiled=True),
        lax.psum_scatter(fourth, "smp", scatter_dimension=0, tiled=True),
    )
    return cross / jnp.sqrt(fourth + 1e-05)


def solution(mesh):
    in_specs = (P("smp", "var"), P("smp"), P())
    out_specs = P(("var", "smp"), None)
    return jax.shard_map(shards, mesh=mesh, in_specs=in_specs, out_specs=out_specs, check_vma=False)
```

profile of v0, /device:TPU:0, one launch (start us, length us, event | category | flops | bytes accessed | tf_op | source)
XLA Modules:
  0.0 185.6 jit_solution(6487847422519628957)
XLA Ops:
  6.5 0.0 reduce-scatter.3.cloned.1.call-start
  6.5 0.5 collective-permute-start
  7.0 15.7 %collective-permute-done = bf16[1024,512]{1,0:T(8,128)(2,1)} collective-permute-done((bf16[1024,512]{1,0:T(8,128)(2,1)}, bf16[1024,512]{1,0:T(8,128)(2,1)}, u32[]{:S(2)}, u32[]{:S(2)}) %collective-permute-start) | collective-permute-done | bytes 1048608 | tf_op jit(solution)/shard_map/ppermute | solution.py:10
  22.7 2.3 %collective-permute-start.1 = (bf16[1024,512]{1,0:T(8,128)(2,1)}, bf16[1024,512]{1,0:T(8,128)(2,1)}, u32[]{:S(2)}, u32[]{:S(2)}) collective-permute-start(bf16[1024,512]{1,0:T(8,128)(2,1)} %collective-permute-done), channel_id=1, source_target_pairs={{0,24},{4,28},{8,0},{12,4},{16,8},{20,12},{24,16},{28,20},{1,25},{... | collective-permute-start | bytes 3145736 | tf_op jit(solution)/shard_map/ppermute | solution.py:10
  25.0 1.3 reduce_sum.18
  26.9 0.7 broadcast_subtract_fusion
  27.6 0.8 select_reduce_fusion
  28.3 0.0 copy-start
  28.4 1.4 constant_dynamic-update-slice_fusion.2
  29.7 1.3 constant_dynamic-update-slice_fusion.1
  31.0 16.0 %collective-permute-done.1 = bf16[1024,512]{1,0:T(8,128)(2,1)} collective-permute-done((bf16[1024,512]{1,0:T(8,128)(2,1)}, bf16[1024,512]{1,0:T(8,128)(2,1)}, u32[]{:S(2)}, u32[]{:S(2)}) %collective-permute-start.1) | collective-permute-done | bytes 1048608 | tf_op jit(solution)/shard_map/ppermute | solution.py:10
  47.1 1.3 constant_dynamic-update-slice_fusion
  48.4 0.0 copy-done
  48.4 3.6 %fusion.4 = f32[512,1536]{1,0:T(8,128)} fusion(bf16[1024,1536]{1,0:T(8,128)(2,1)S(1)} %constant_dynamic-update-slice_fusion, bf16[1024,512]{1,0:T(8,128)(2,1)S(1)} %copy-done, f32[1024]{0:T(1024)S(1)} %select_reduce_fusion), kind=kOutput, calls=%fused_computation.6 | convolution fusion | flops 1612185600 | bytes 7344128 | tf_op jit(solution)/shard_map/dot_general | solution.py:27
  52.0 0.0 reduce-scatter.3.cloned.1.call-update
  52.0 0.0 reduce-scatter.5.cloned.1.call-start
  52.0 4.8 %fusion = f32[512,1536]{1,0:T(8,128)} fusion(bf16[1024,1536]{1,0:T(8,128)(2,1)S(1)} %constant_dynamic-update-slice_fusion, bf16[1024,512]{1,0:T(8,128)(2,1)} %param.3), kind=kOutput, calls=%fused_computation.1 | convolution fusion | flops 1616904192 | bytes 7340032 | tf_op jit(solution)/shard_map/dot_general | solution.py:28
  56.8 0.0 reduce-scatter.5.cloned.1.call-update
  56.8 56.9 %reduce-scatter.3.cloned.1.call-done = f32[128,1536]{1,0:T(8,128)} async-done(((f32[512,1536]{1,0:T(8,128)}), f32[128,1536]{1,0:T(8,128)}) %reduce-scatter.3.cloned.1.call-update) | async-done | bytes 786448 | tf_op jit(solution)/shard_map/reduce_scatter | solution.py:30
  113.7 62.6 %reduce-scatter.5.cloned.1.call-done = f32[128,1536]{1,0:T(8,128)} async-done(((f32[512,1536]{1,0:T(8,128)}), f32[128,1536]{1,0:T(8,128)}) %reduce-scatter.5.cloned.1.call-update) | async-done | bytes 786448 | tf_op jit(solution)/shard_map/reduce_scatter | solution.py:31
  176.4 2.4 %rsqrt_multiply_fusion = f32[128,1536]{1,0:T(8,128)} fusion(f32[128,1536]{1,0:T(8,128)} %reduce-scatter.3.cloned.1.call-done, f32[128,1536]{1,0:T(8,128)} %reduce-scatter.5.cloned.1.call-done), kind=kLoop, calls=%fused_computation.8 | loop fusion | flops 393216 | bytes 2359296 | tf_op jit(solution)/shard_map/div | solution.py:33
Async XLA Ops:
  6.5 107.2 %reduce-scatter.3.cloned.1.call-start = ((), (), s32[]{:S(2)}) async-start(), calls=%async_computation.2 | async-start | bytes 3932160 | tf_op jit(solution)/shard_map/reduce_scatter | solution.py:30
  6.5 16.2 %collective-permute-start = (bf16[1024,512]{1,0:T(8,128)(2,1)}, bf16[1024,512]{1,0:T(8,128)(2,1)}, u32[]{:S(2)}, u32[]{:S(2)}) collective-permute-start(bf16[1024,512]{1,0:T(8,128)(2,1)} %param.3), channel_id=1, source_target_pairs={{0,4},{4,8},{8,12},{12,16},{16,20},{20,24},{24,28},{28,0},{1,5},{5... | collective-permute-start | bytes 3145736 | tf_op jit(solution)/shard_map/ppermute | solution.py:10
  22.7 24.4 %collective-permute-start.1 = (bf16[1024,512]{1,0:T(8,128)(2,1)}, bf16[1024,512]{1,0:T(8,128)(2,1)}, u32[]{:S(2)}, u32[]{:S(2)}) collective-permute-start(bf16[1024,512]{1,0:T(8,128)(2,1)} %collective-permute-done), channel_id=1, source_target_pairs={{0,24},{4,28},{8,0},{12,4},{16,8},{20,12},{24,16},{28,20},{1,25},{... | collective-permute-start | bytes 3145736 | tf_op jit(solution)/shard_map/ppermute | solution.py:10
  28.3 20.0 %copy-start = (bf16[1024,512]{1,0:T(8,128)(2,1)S(1)}, bf16[1024,512]{1,0:T(8,128)(2,1)}, u32[]{:S(2)}) copy-start(bf16[1024,512]{1,0:T(8,128)(2,1)} %param.3) | copy-start | bytes 3145732
  52.0 124.4 %reduce-scatter.5.cloned.1.call-start = ((), (), s32[]{:S(2)}) async-start(), calls=%async_computation.3 | async-start | bytes 3932160 | tf_op jit(solution)/shard_map/reduce_scatter | solution.py:31
Sparse Core Ops, SparseCore 0:
  52.1 61.5 reduce-scatter.2
  116.0 60.3 reduce-scatter.4
where the time goes:
time: 186 us
  waiting for transfers between devices  151 us (81%)
  between operations  14.1 us (8%)
  matrix products  8.37 us (4%)
  other arithmetic  5.05 us (3%)
  local copies, waits for them, and re-layouts  3.98 us (2%)
  starting transfers between devices  2.84 us (2%)
    reduce_scatter x1, waiting for transfers between devices, shards(): lax.psum_scatter(fourth, 'smp', scatter_dimension=0, tiled=True)  62.6 us
    reduce_scatter x1, waiting for transfers between devices, shards(): lax.psum_scatter(cross, 'smp', scatter_dimension=0, tiled=True)  56.9 us
    ppermute x2, waiting for transfers between devices, from_behind(): return lax.ppermute(value, axis, pairs)  31.7 us
    dot_general x1, matrix products, shards(): lax.dot_general(squared, right_sq, contract, preferred_element_type=jnp.f...  4.78 us
  transfers between devices with their start and end apart: 4, of which 4 were waited for; matrix products, arithmetic and copies ran while one was open for 5% of the time, Pallas kernels for 0%

commit v1 on v0

v1 whole, which is shorter than its diff:
```python
import functools

import jax
import jax.numpy as jnp
from jax import lax
from jax.experimental import pallas as pl
from jax.experimental.pallas import tpu as pltpu
from jax.sharding import PartitionSpec as P

MESH = pl.DeviceIdType.MESH
F32, BF16 = jnp.float32, jnp.bfloat16


def kernel(
    nv, n, d_ref, class_ref, effect_ref, out_ref,
    after, wt, qt, sq, part, wire, relay, fwd, summed, direct, turned, before,
    d_send, d_recv, relay_send, relay_recv, fwd_send, sum_recv, dir_send, dir_recv, t_send, t_recv,
):
    depth, width = d_ref.shape
    rows = width // n
    pairs = n // 2
    v, s = lax.axis_index("var"), lax.axis_index("smp")
    nxt, prv = lax.rem(v + 1, nv), lax.rem(v + nv - 1, nv)
    pair, odd = s // 2, lax.rem(s, 2)
    partner = s + 1 - 2 * odd

    barrier = pltpu.get_barrier_semaphore()
    for step in range(1, n):
        pl.semaphore_signal(barrier, inc=1, device_id=(v, lax.rem(s + step, n)), device_id_type=MESH)
    for step in range(n):
        for near in (nxt, prv):
            pl.semaphore_signal(barrier, inc=1, device_id=(near, lax.rem(s + step, n)), device_id_type=MESH)
    pl.semaphore_wait(barrier, 3 * n - 1)

    shift = pltpu.make_async_remote_copy(
        src_ref=d_ref, dst_ref=after, send_sem=d_send, recv_sem=d_recv,
        device_id=(prv, s), device_id_type=MESH,
    )
    shift.start()

    classes = effect_ref.shape[0]
    mean = effect_ref[0]
    for c in range(1, classes):
        mean = mean + effect_ref[c]
    mean = mean / classes
    picked = class_ref[...]
    trait = jnp.zeros(picked.shape, F32)
    for c in range(classes):
        trait = jnp.where(picked == c, effect_ref[c] - mean, trait)
    for at in range(0, width, 128):
        cols = d_ref[:, at:at + 128].astype(F32).T
        wt[at:at + 128, :] = (cols * trait).astype(BF16)
        qt[at:at + 128, :] = (cols * cols).astype(BF16)

    def squares(ref):
        values = ref[...].astype(F32)
        sq[...] = (values * values).astype(BF16)

    def at_rows(index, count=1):
        return pl.ds(pl.multiple_of(index * rows, rows), count * rows)

    def relay_copy(u, k):
        other = lax.rem(pair + k, pairs)
        return pltpu.make_async_remote_copy(
            src_ref=wire.at[u, at_rows(2 * other, 2)], dst_ref=relay.at[u, k - 1],
            send_sem=relay_send.at[u, k - 1], recv_sem=relay_recv.at[u, k - 1],
            device_id=(v, partner), device_id_type=MESH,
        )

    def fwd_copy(u, k, j):
        other = lax.rem(pair + k, pairs)
        return pltpu.make_async_remote_copy(
            src_ref=fwd.at[u, k - 1, j], dst_ref=summed.at[u, pairs - k - 1],
            send_sem=fwd_send.at[u, k - 1, j], recv_sem=sum_recv.at[u, pairs - k - 1],
            device_id=(v, 2 * other + j), device_id_type=MESH,
        )

    def dir_copy(u):
        return pltpu.make_async_remote_copy(
            src_ref=wire.at[u, at_rows(partner)], dst_ref=direct.at[u],
            send_sem=dir_send.at[u], recv_sem=dir_recv.at[u],
            device_id=(v, partner), device_id_type=MESH,
        )

    def outer(k):
        higher = lax.rem(pair + k, pairs) > pair
        return jnp.logical_or(
            jnp.logical_and(higher, odd == 0), jnp.logical_and(jnp.logical_not(higher), odd == 1)
        )

    def product(u, left, right):
        got = jnp.dot(left[...], right[...], preferred_element_type=F32)
        part[u] = got
        wire[u] = got.astype(BF16)

    def send_relays(u):
        for k in range(1, pairs):
            @pl.when(outer(k))
            def _():
                relay_copy(u, k).start()

    def send_sums(u):
        for k in range(1, pairs):
            @pl.when(jnp.logical_not(outer(k)))
            def _():
                relay_copy(u, k).wait_recv()
                other = lax.rem(pair + k, pairs)
                for j in range(2):
                    own = part[u, at_rows(2 * other + j), :]
                    got = relay[u, k - 1, j * rows:(j + 1) * rows, :].astype(F32)
                    fwd[u, k - 1, j] = (own + got).astype(BF16)
                    fwd_copy(u, k, j).start()

    def total(u):
        got = part[u, at_rows(s), :]
        dir_copy(u).wait_recv()
        got = got + direct[u].astype(F32)
        for k in range(1, pairs):
            fwd_copy(u, k, 0).wait_recv()
            got = got + summed[u, pairs - k - 1].astype(F32)
        return got

    product(0, wt, d_ref)
    send_relays(0)
    squares(d_ref)
    product(1, qt, sq)
    send_relays(1)
    dir_copy(0).start()
    dir_copy(1).start()
    shift.wait_recv()
    product(2, wt, after)
    send_relays(2)
    squares(after)
    product(3, qt, sq)
    send_relays(3)
    dir_copy(2).start()
    dir_copy(3).start()
    for u in range(4):
        send_sums(u)

    cross = total(2)
    fourth = total(3)
    stat = cross / jnp.sqrt(fourth + 1e-05)
    out_ref[:, 2 * width:] = stat
    turned[...] = stat.T.astype(BF16)

    def turn_copy(t):
        return pltpu.make_async_remote_copy(
            src_ref=turned.at[t * rows:(t + 1) * rows], dst_ref=before.at[s],
            send_sem=t_send.at[t], recv_sem=t_recv.at[s],
            device_id=(nxt, t), device_id_type=MESH,
        )

    def turn_wait(t):
        return pltpu.make_async_remote_copy(
            src_ref=turned.at[t * rows:(t + 1) * rows], dst_ref=before.at[t],
            send_sem=t_send.at[t], recv_sem=t_recv.at[t],
            device_id=(nxt, t), device_id_type=MESH,
        )

    for t in range(n):
        turn_copy(t).start()
    cross = total(0)
    fourth = total(1)
    out_ref[:, width:2 * width] = cross / jnp.sqrt(fourth + 1e-05)
    for t in range(n):
        turn_wait(t).wait_recv()
        out_ref[:, t * rows:(t + 1) * rows] = before[t].astype(F32)

    shift.wait_send()
    for u in range(4):
        dir_copy(u).wait_send()
        for k in range(1, pairs):
            @pl.when(outer(k))
            def _():
                relay_copy(u, k).wait_send()

            @pl.when(jnp.logical_not(outer(k)))
            def _():
                for j in range(2):
                    fwd_copy(u, k, j).wait_send()
    for t in range(n):
        turn_wait(t).wait_send()


def solution(mesh):
    nv, n = mesh.shape["var"], mesh.shape["smp"]

    def shards(dosage, trait_class, class_effect):
        depth, width = dosage.shape
        rows, far = width // n, max(n // 2 - 1, 1)
        dma = pltpu.SemaphoreType.DMA
        return pl.pallas_call(
            functools.partial(kernel, nv, n),
            out_shape=jax.ShapeDtypeStruct((rows, 3 * width), F32),
            in_specs=[
                pl.BlockSpec(memory_space=pltpu.VMEM),
                pl.BlockSpec(memory_space=pltpu.VMEM),
                pl.BlockSpec(memory_space=pltpu.SMEM),
            ],
            out_specs=pl.BlockSpec(memory_space=pltpu.VMEM),
            scratch_shapes=[
                pltpu.VMEM((depth, width), BF16),
                pltpu.VMEM((width, depth), BF16),
                pltpu.VMEM((width, depth), BF16),
                pltpu.VMEM((depth, width), BF16),
                pltpu.VMEM((4, width, width), F32),
                pltpu.VMEM((4, width, width), BF16),
                pltpu.VMEM((4, far, 2 * rows, width), BF16),
                pltpu.VMEM((4, far, 2, rows, width), BF16),
                pltpu.VMEM((4, far, rows, width), BF16),
                pltpu.VMEM((4, rows, width), BF16),
                pltpu.VMEM((width, rows), BF16),
                pltpu.VMEM((n, rows, rows), BF16),
                dma, dma,
                dma((4, far)), dma((4, far)),
                dma((4, far, 2)), dma((4, far)),
                dma((4,)), dma((4,)),
                dma((n,)), dma((n,)),
            ],
            compiler_params=pltpu.CompilerParams(
                collective_id=0, has_side_effects=True, vmem_limit_bytes=60 * 1024 * 1024
            ),
        )(dosage, trait_class.reshape(1, depth), class_effect)

    in_specs = (P("smp", "var"), P("smp"), P())
    out_specs = P(("var", "smp"), None)
    return jax.shard_map(shards, mesh=mesh, in_specs=in_specs, out_specs=out_specs, check_vma=False)
```

time: 186 us -> 54 us (0.29)
  the two profiles are of different devices: /device:TPU:0 before, /device:TPU:5 now
where the time goes in v1:
time: 54 us; the launch traced here: 53.8 us
  Pallas kernels  51.7 us (96%)
  local copies, waits for them, and re-layouts  2.07 us (4%)
    pallas_call x1, Pallas kernels, shards(): pl.pallas_call(functools.partial(kernel, nv, n), out_shape=jax.ShapeDtype...  51.7 us
    unnamed x1, local copies, waits for them, and re-layouts  2.07 us

profile of v1, /device:TPU:5, one launch (start us, length us, event | category | flops | bytes accessed | tf_op | source)
XLA Modules:
  0.0 53.8 jit_solution(572231619232970080)
XLA Ops:
  0.0 51.7 %shard_map.37 = f32[128,1536]{1,0:T(8,128)} custom-call(bf16[1024,512]{1,0:T(8,128)(2,1)} %d_ref.1, s32[1,1024]{1,0:T(1,128)} %bitcast.1, f32[16]{0:T(128)} %effect_ref.1), custom_call_target="tpu_custom_call" | custom-call | tf_op jit(solution)/shard_map/pallas_call | solution.py:193
  51.7 2.1 %copy.5 = f32[128,1536]{1,0:T(8,128)} copy(f32[128,1536]{1,0:T(8,128)} %shard_map.37) | data formatting | bytes 1572864

commit v2 on v1

--- a/solution.py
+++ b/solution.py
@@ -32,11 +32,20 @@
             pl.semaphore_signal(barrier, inc=1, device_id=(near, lax.rem(s + step, n)), device_id_type=MESH)
     pl.semaphore_wait(barrier, 3 * n - 1)
 
-    shift = pltpu.make_async_remote_copy(
-        src_ref=d_ref, dst_ref=after, send_sem=d_send, recv_sem=d_recv,
-        device_id=(prv, s), device_id_type=MESH,
-    )
-    shift.start()
+    half = width // 2
+
+    def cols(h):
+        return slice(h * half, (h + 1) * half)
+
+    def shift(h):
+        return pltpu.make_async_remote_copy(
+            src_ref=d_ref.at[:, cols(h)], dst_ref=after.at[:, cols(h)],
+            send_sem=d_send.at[h], recv_sem=d_recv.at[h],
+            device_id=(prv, s), device_id_type=MESH,
+        )
+
+    for h in range(2):
+        shift(h).start()
 
     classes = effect_ref.shape[0]
     mean = effect_ref[0]
@@ -48,13 +57,9 @@
     for c in range(classes):
         trait = jnp.where(picked == c, effect_ref[c] - mean, trait)
     for at in range(0, width, 128):
-        cols = d_ref[:, at:at + 128].astype(F32).T
-        wt[at:at + 128, :] = (cols * trait).astype(BF16)
-        qt[at:at + 128, :] = (cols * cols).astype(BF16)
-
-    def squares(ref):
-        values = ref[...].astype(F32)
-        sq[...] = (values * values).astype(BF16)
+        values = d_ref[:, at:at + 128].astype(F32).T
+        wt[at:at + 128, :] = (values * trait).astype(BF16)
+        qt[at:at + 128, :] = (values * values).astype(BF16)
 
     def at_rows(index, count=1):
         return pl.ds(pl.multiple_of(index * rows, rows), count * rows)
@@ -88,10 +93,18 @@
             jnp.logical_and(higher, odd == 0), jnp.logical_and(jnp.logical_not(higher), odd == 1)
         )
 
-    def product(u, left, right):
-        got = jnp.dot(left[...], right[...], preferred_element_type=F32)
+    def products(block, h):
+        right = (after if block else d_ref)[:, cols(h)]
+        u = 4 * block + 2 * h
+        product(u, jnp.dot(wt[...], right, preferred_element_type=F32))
+        values = right.astype(F32)
+        sq[...] = (values * values).astype(BF16)
+        product(u + 1, jnp.dot(qt[...], sq[...], preferred_element_type=F32))
+
+    def product(u, got):
         part[u] = got
         wire[u] = got.astype(BF16)
+        send_relays(u)
 
     def send_relays(u):
         for k in range(1, pairs):
@@ -120,29 +133,20 @@
             got = got + summed[u, pairs - k - 1].astype(F32)
         return got
 
-    product(0, wt, d_ref)
-    send_relays(0)
-    squares(d_ref)
-    product(1, qt, sq)
-    send_relays(1)
-    dir_copy(0).start()
-    dir_copy(1).start()
-    shift.wait_recv()
-    product(2, wt, after)
-    send_relays(2)
-    squares(after)
-    product(3, qt, sq)
-    send_relays(3)
-    dir_copy(2).start()
-    dir_copy(3).start()
+    for h in range(2):
+        products(0, h)
+    shift(0).wait_recv()
+    products(1, 0)
+    send_sums(0)
+    send_sums(1)
+    shift(1).wait_recv()
+    products(1, 1)
+    for u in range(4, 8):
+        dir_copy(u).start()
     for u in range(4):
+        dir_copy(u).start()
+    for u in range(2, 8):
         send_sums(u)
-
-    cross = total(2)
-    fourth = total(3)
-    stat = cross / jnp.sqrt(fourth + 1e-05)
-    out_ref[:, 2 * width:] = stat
-    turned[...] = stat.T.astype(BF16)
 
     def turn_copy(t):
         return pltpu.make_async_remote_copy(
@@ -158,17 +162,22 @@
             device_id=(nxt, t), device_id_type=MESH,
         )
 
-    for t in range(n):
-        turn_copy(t).start()
-    cross = total(0)
-    fourth = total(1)
-    out_ref[:, width:2 * width] = cross / jnp.sqrt(fourth + 1e-05)
+    for h in range(2):
+        stat = total(4 + 2 * h) / jnp.sqrt(total(5 + 2 * h) + 1e-05)
+        out_ref[:, 2 * width + h * half:2 * width + (h + 1) * half] = stat
+        turned[cols(h), :] = stat.T.astype(BF16)
+        for t in range(h * pairs, (h + 1) * pairs):
+            turn_copy(t).start()
+    for h in range(2):
+        stat = total(2 * h) / jnp.sqrt(total(2 * h + 1) + 1e-05)
+        out_ref[:, width + h * half:width + (h + 1) * half] = stat
     for t in range(n):
         turn_wait(t).wait_recv()
         out_ref[:, t * rows:(t + 1) * rows] = before[t].astype(F32)
 
-    shift.wait_send()
-    for u in range(4):
+    for h in range(2):
+        shift(h).wait_send()
+    for u in range(8):
         dir_copy(u).wait_send()
         for k in range(1, pairs):
             @pl.when(outer(k))
@@ -188,7 +197,7 @@
 
     def shards(dosage, trait_class, class_effect):
         depth, width = dosage.shape
-        rows, far = width // n, max(n // 2 - 1, 1)
+        rows, half, far = width // n, width // 2, max(n // 2 - 1, 1)
         dma = pltpu.SemaphoreType.DMA
         return pl.pallas_call(
             functools.partial(kernel, nv, n),
@@ -203,23 +212,23 @@
                 pltpu.VMEM((depth, width), BF16),
                 pltpu.VMEM((width, depth), BF16),
                 pltpu.VMEM((width, depth), BF16),
-                pltpu.VMEM((depth, width), BF16),
-                pltpu.VMEM((4, width, width), F32),
-                pltpu.VMEM((4, width, width), BF16),
-                pltpu.VMEM((4, far, 2 * rows, width), BF16),
-                pltpu.VMEM((4, far, 2, rows, width), BF16),
-                pltpu.VMEM((4, far, rows, width), BF16),
-                pltpu.VMEM((4, rows, width), BF16),
+                pltpu.VMEM((depth, half), BF16),
+                pltpu.VMEM((8, width, half), F32),
+                pltpu.VMEM((8, width, half), BF16),
+                pltpu.VMEM((8, far, 2 * rows, half), BF16),
+                pltpu.VMEM((8, far, 2, rows, half), BF16),
+                pltpu.VMEM((8, far, rows, half), BF16),
+                pltpu.VMEM((8, rows, half), BF16),
                 pltpu.VMEM((width, rows), BF16),
                 pltpu.VMEM((n, rows, rows), BF16),
-                dma, dma,
-                dma((4, far)), dma((4, far)),
-                dma((4, far, 2)), dma((4, far)),
-                dma((4,)), dma((4,)),
+                dma((2,)), dma((2,)),
+                dma((8, far)), dma((8, far)),
+                dma((8, far, 2)), dma((8, far)),
+                dma((8,)), dma((8,)),
                 dma((n,)), dma((n,)),
             ],
             compiler_params=pltpu.CompilerParams(
-                collective_id=0, has_side_effects=True, vmem_limit_bytes=60 * 1024 * 1024
+                collective_id=0, has_side_effects=True, vmem_limit_bytes=20 * 1024 * 1024
             ),
         )(dosage, trait_class.reshape(1, depth), class_effect)
 

time: 54 us -> 47.9 us (0.89)
  the two profiles are of different devices: /device:TPU:5 before, /device:TPU:0 now
where the time goes in v2:
time: 47.9 us; the launch traced here: 47.7 us
  Pallas kernels  44.3 us (92%)
  local copies, waits for them, and re-layouts  3.45 us (7%)
    pallas_call x1, Pallas kernels, shards(): pl.pallas_call(functools.partial(kernel, nv, n), out_shape=jax.ShapeDtype...  44.3 us
    unnamed x7, local copies, waits for them, and re-layouts  3.45 us

profile of v2, /device:TPU:0, one launch (start us, length us, event | category | flops | bytes accessed | tf_op | source)
XLA Modules:
  0.0 47.7 jit_solution(92693157755651031)
XLA Ops:
  0.0 0.0 copy-start.2
  0.0 0.7 %copy-done.2 = f32[16]{0:T(128)S(1)} copy-done((f32[16]{0:T(128)S(1)}, f32[16]{0:T(128)}, u32[]{:S(2)}) %copy-start.2) | copy-done | bytes 88
  0.7 0.0 copy-start
  0.7 1.2 %copy-done = bf16[1024,512]{1,0:T(8,128)(2,1)S(1)} copy-done((bf16[1024,512]{1,0:T(8,128)(2,1)S(1)}, bf16[1024,512]{1,0:T(8,128)(2,1)}, u32[]{:S(2)}) %copy-start) | copy-done | bytes 1048600
  1.9 0.0 copy-start.1
  1.9 0.7 %copy-done.1 = s32[1024]{0:T(1024)S(1)} copy-done((s32[1024]{0:T(1024)S(1)}, s32[1024]{0:T(1024)}, u32[]{:S(2)}) %copy-start.1) | copy-done | bytes 4120
  2.6 44.3 %shard_map.37 = f32[128,1536]{1,0:T(8,128)S(1)} custom-call(bf16[1024,512]{1,0:T(8,128)(2,1)S(1)} %copy-done, s32[1,1024]{1,0:T(1,128)S(1)} %bitcast.1, f32[16]{0:T(128)S(1)} %copy-done.2), custom_call_target="tpu_custom_call" | custom-call | tf_op jit(solution)/shard_map/pallas_call | solution.py:202
  46.9 0.9 %copy.5 = f32[128,1536]{1,0:T(8,128)} copy(f32[128,1536]{1,0:T(8,128)S(1)} %shard_map.37) | data formatting | bytes 1572864
Async XLA Ops:
  0.0 0.7 %copy-start.2 = (f32[16]{0:T(128)S(1)}, f32[16]{0:T(128)}, u32[]{:S(2)}) copy-start(f32[16]{0:T(128)} %effect_ref.1) | copy-start | bytes 196
  0.7 1.2 %copy-start = (bf16[1024,512]{1,0:T(8,128)(2,1)S(1)}, bf16[1024,512]{1,0:T(8,128)(2,1)}, u32[]{:S(2)}) copy-start(bf16[1024,512]{1,0:T(8,128)(2,1)} %d_ref.1) | copy-start | bytes 3145732
  1.9 0.7 %copy-start.1 = (s32[1024]{0:T(1024)S(1)}, s32[1024]{0:T(1024)}, u32[]{:S(2)}) copy-start(s32[1024]{0:T(1024)} %param.4) | copy-start | bytes 12292

commit v3 on v0

v3 whole, which is shorter than its diff:
```python
import functools

import jax
import jax.numpy as jnp
from jax import lax
from jax.experimental import pallas as pl
from jax.experimental.pallas import tpu as pltpu
from jax.sharding import PartitionSpec as P

MESH = pl.DeviceIdType.MESH
F32, BF16 = jnp.float32, jnp.bfloat16
LANES = 128


def kernel(
    nv, n, dosage_ref, class_hbm, effect_hbm, out_ref,
    d_ref, class_ref, effect_ref, after, wt, qt, sq, turned, before, own_turned, mirrored,
    own_part, own_wire, own_relay, own_fwd, own_summed, own_direct,
    next_part, next_wire, next_relay, next_fwd, next_summed, next_direct,
    load_sem, d_send, d_recv, t_send, t_recv, m_send, m_recv,
    own_rs, own_rr, own_fs, own_sr, own_ds, own_dr,
    next_rs, next_rr, next_fs, next_sr, next_ds, next_dr,
):
    depth, width = d_ref.shape
    rows, half, pairs = width // n, width // 2, n // 2
    fold = rows % LANES == 0
    v, s = lax.axis_index("var"), lax.axis_index("smp")
    nxt, prv = lax.rem(v + 1, nv), lax.rem(v + nv - 1, nv)
    pair, odd = s // 2, lax.rem(s, 2)
    partner = s + 1 - 2 * odd

    loads = [
        pltpu.make_async_copy(dosage_ref, d_ref, load_sem.at[0]),
        pltpu.make_async_copy(class_hbm, class_ref, load_sem.at[1]),
        pltpu.make_async_copy(effect_hbm, effect_ref, load_sem.at[2]),
    ]
    for load in loads:
        load.start()
    barrier = pltpu.get_barrier_semaphore()
    for near in (nxt, prv):
        for step in range(n):
            pl.semaphore_signal(barrier, inc=1, device_id=(near, lax.rem(s + step, n)), device_id_type=MESH)
    for step in range(1, n):
        pl.semaphore_signal(barrier, inc=1, device_id=(v, lax.rem(s + step, n)), device_id_type=MESH)
    for load in loads:
        load.wait()
    pl.semaphore_wait(barrier, 3 * n - 1)

    def cols(h):
        return slice(h * half, (h + 1) * half)

    def shift(h):
        return pltpu.make_async_remote_copy(
            src_ref=d_ref.at[:, cols(h)], dst_ref=after.at[:, cols(h)],
            send_sem=d_send.at[h], recv_sem=d_recv.at[h],
            device_id=(prv, s), device_id_type=MESH,
        )

    for h in range(2):
        shift(h).start()

    classes = effect_ref.shape[0]
    mean = effect_ref[0]
    for c in range(1, classes):
        mean = mean + effect_ref[c]
    mean = mean / classes
    picked = class_ref[...]
    trait = jnp.zeros(picked.shape, F32)
    for c in range(classes):
        trait = jnp.where(picked == c, effect_ref[c] - mean, trait)
    for at in range(0, width, LANES):
        values = d_ref[:, at:at + LANES].astype(F32).T
        wt[at:at + LANES, :] = (values * trait).astype(BF16)
        qt[at:at + LANES, :] = (values * values).astype(BF16)

    def owns(a, c):
        from_a, from_c = abs_of(2 * a - (n - 1)), abs_of(2 * c - (n - 1))
        return jnp.logical_or(from_a > from_c, jnp.logical_and(from_a == from_c, a < c))

    def abs_of(x):
        return lax.max(x, -x) if isinstance(x, jax.Array) else jnp.int32(abs(x))

    def extent(t):
        if not fold:
            return slice(0, width)
        first, last = (t, n - 1 - t) if t < pairs else (n - t, t)
        return slice(first * rows, (last + 1) * rows)

    def cases(index, count, body):
        for known in range(count):
            pl.when(index == known)(functools.partial(body, known))

    def at_rows(index):
        return pl.ds(pl.multiple_of(index * rows, rows), rows)

    def outer(k):
        higher = lax.rem(pair + k, pairs) > pair
        return jnp.logical_or(
            jnp.logical_and(higher, odd == 0), jnp.logical_and(jnp.logical_not(higher), odd == 1)
        )

    class Group:
        def __init__(self, folded, part, wire, relay, fwd, summed, direct, rs, rr, fs, sr, ds, dr):
            self.folded, self.part, self.wire, self.relay = folded, part, wire, relay
            self.fwd, self.summed, self.direct = fwd, summed, direct
            self.rs, self.rr, self.fs, self.sr, self.ds, self.dr = rs, rr, fs, sr, ds, dr

        def span(self, t):
            return extent(t) if self.folded else slice(None)

        def by(self, index, count, body):
            if self.folded:
                cases(index, count, body)
            else:
                body(index)

        def relay_copy(self, u, other, j):
            t = 2 * other + j
            span = self.span(t)
            return pltpu.make_async_remote_copy(
                src_ref=self.wire.at[u, at_rows(t), span], dst_ref=self.relay.at[u, other, j, :, span],
                send_sem=self.rs.at[u, other, j], recv_sem=self.rr.at[u, other, j],
                device_id=(v, partner), device_id_type=MESH,
            )

        def fwd_copy(self, u, other, j):
            t = 2 * other + j
            span = self.span(t)
            return pltpu.make_async_remote_copy(
                src_ref=self.fwd.at[u, other, j, :, span], dst_ref=self.summed.at[u, pair, :, span],
                send_sem=self.fs.at[u, other, j], recv_sem=self.sr.at[u, pair],
                device_id=(v, t), device_id_type=MESH,
            )

        def sum_wait(self, u, source, t):
            span = self.span(t)
            here = self.summed.at[u, source, :, span]
            pltpu.make_async_remote_copy(
                src_ref=here, dst_ref=here, send_sem=self.fs.at[u, source, 0], recv_sem=self.sr.at[u, source],
                device_id=(v, partner), device_id_type=MESH,
            ).wait_recv()

        def dir_copy(self, u, t):
            span = self.span(t)
            return pltpu.make_async_remote_copy(
                src_ref=self.wire.at[u, at_rows(t), span], dst_ref=self.direct.at[u, :, span],
                send_sem=self.ds.at[u], recv_sem=self.dr.at[u],
                device_id=(v, partner), device_id_type=MESH,
            )

        def product(self, u, left, right):
            got = jnp.dot(left[...], right, preferred_element_type=F32)
            self.part[u] = got
            self.wire[u] = got.astype(BF16)
            for k in range(1, pairs):
                @pl.when(outer(k))
                def _():
                    def send(other):
                        for j in range(2):
                            self.relay_copy(u, other, j).start()

                    self.by(lax.rem(pair + k, pairs), pairs, send)

        def send_sums(self, u):
            for k in range(1, pairs):
                @pl.when(jnp.logical_not(outer(k)))
                def _():
                    def send(other):
                        for j in range(2):
                            self.relay_copy(u, other, j).wait_recv()
                            own = self.part[u, at_rows(2 * other + j), :]
                            self.fwd[u, other, j] = (own + self.relay[u, other, j].astype(F32)).astype(BF16)
                            self.fwd_copy(u, other, j).start()

                    self.by(lax.rem(pair + k, pairs), pairs, send)

        def send_direct(self, u):
            self.by(partner, n, lambda t: self.dir_copy(u, t).start())

        def total(self, u):
            def wait(t):
                self.dir_copy(u, t).wait_recv()
                for k in range(1, pairs):
                    self.sum_wait(u, lax.rem(pair + k, pairs), t)

            self.by(s, n, wait)
            got = self.part[u, at_rows(s), :] + self.direct[u].astype(F32)
            for k in range(1, pairs):
                got = got + self.summed[u, lax.rem(pair + k, pairs)].astype(F32)
            return got

        def finish(self, units):
            for u in range(units):
                self.by(partner, n, lambda t: self.dir_copy(u, t).wait_send())
                for k in range(1, pairs):
                    def relays(other):
                        for j in range(2):
                            self.relay_copy(u, other, j).wait_send()

                    def sums(other):
                        for j in range(2):
                            self.fwd_copy(u, other, j).wait_send()

                    other = lax.rem(pair + k, pairs)

                    @pl.when(outer(k))
                    def _():
                        self.by(other, pairs, relays)

                    @pl.when(jnp.logical_not(outer(k)))
                    def _():
                        self.by(other, pairs, sums)

    own = Group(
        fold, own_part, own_wire, own_relay, own_fwd, own_summed, own_direct,
        own_rs, own_rr, own_fs, own_sr, own_ds, own_dr,
    )
    follow = Group(
        False, next_part, next_wire, next_relay, next_fwd, next_summed, next_direct,
        next_rs, next_rr, next_fs, next_sr, next_ds, next_dr,
    )

    def squares(values):
        values = values.astype(F32)
        return (values * values).astype(BF16)

    own.product(0, wt, d_ref[...])
    sq[...] = squares(d_ref[...])
    own.product(1, qt, sq[...])
    for h in range(2):
        shift(h).wait_recv()
        follow.product(2 * h, wt, after[:, cols(h)])
        sq[:, cols(h)] = squares(after[:, cols(h)])
        follow.product(2 * h + 1, qt, sq[:, cols(h)])
        if h == 0:
            for u in range(2):
                own.send_sums(u)
    for u in range(4):
        follow.send_direct(u)
    for u in range(2):
        own.send_direct(u)
    for u in range(4):
        follow.send_sums(u)

    def turn_copy(t, slot):
        return pltpu.make_async_remote_copy(
            src_ref=turned.at[t * rows:(t + 1) * rows], dst_ref=before.at[slot],
            send_sem=t_send.at[t], recv_sem=t_recv.at[slot],
            device_id=(nxt, t), device_id_type=MESH,
        )

    def mirror_copy(t, slot):
        return pltpu.make_async_remote_copy(
            src_ref=own_turned.at[t * rows:(t + 1) * rows], dst_ref=mirrored.at[slot],
            send_sem=m_send.at[t], recv_sem=m_recv.at[slot],
            device_id=(v, t), device_id_type=MESH,
        )

    for h in range(2):
        stat = follow.total(2 * h) / jnp.sqrt(follow.total(2 * h + 1) + 1e-05)
        out_ref[:, 2 * width + h * half:2 * width + (h + 1) * half] = stat
        turned[cols(h), :] = stat.T.astype(BF16)
        for t in range(h * pairs, (h + 1) * pairs):
            turn_copy(t, s).start()
    stat = own.total(0) / jnp.sqrt(own.total(1) + 1e-05)
    if fold:
        own_turned[...] = stat.T.astype(BF16)
        for t in range(n):
            @pl.when(owns(s, t))
            def _():
                mirror_copy(t, s).start()
    out_ref[:, width:2 * width] = stat
    for t in range(n):
        turn_copy(t, t).wait_recv()
        out_ref[:, t * rows:(t + 1) * rows] = before[t].astype(F32)
    if fold:
        for t in range(n):
            @pl.when(owns(t, s))
            def _():
                mirror_copy(t, t).wait_recv()
                out_ref[:, width + t * rows:width + (t + 1) * rows] = mirrored[t].astype(F32)

            @pl.when(owns(s, t))
            def _():
                mirror_copy(t, t).wait_send()

    for h in range(2):
        shift(h).wait_send()
    own.finish(2)
    follow.finish(4)
    for t in range(n):
        turn_copy(t, t).wait_send()


def solution(mesh):
    nv, n = mesh.shape["var"], mesh.shape["smp"]

    def shards(dosage, trait_class, class_effect):
        depth, width = dosage.shape
        rows, half, pairs = width // n, width // 2, n // 2
        dma, vmem = pltpu.SemaphoreType.DMA, pltpu.VMEM

        def buffers(units, wide):
            return [
                vmem((units, width, wide), F32),
                vmem((units, width, wide), BF16),
                vmem((units, pairs, 2, rows, wide), BF16),
                vmem((units, pairs, 2, rows, wide), BF16),
                vmem((units, pairs, rows, wide), BF16),
                vmem((units, rows, wide), BF16),
            ]

        def semaphores(units):
            return [
                dma((units, pairs, 2)), dma((units, pairs, 2)), dma((units, pairs, 2)),
                dma((units, pairs)), dma((units,)), dma((units,)),
            ]

        return pl.pallas_call(
            functools.partial(kernel, nv, n),
            out_shape=jax.ShapeDtypeStruct((rows, 3 * width), F32),
            in_specs=[pl.BlockSpec(memory_space=pltpu.HBM)] * 3,
            out_specs=pl.BlockSpec(memory_space=vmem),
            scratch_shapes=[
                vmem((depth, width), BF16),
                vmem((1, depth), jnp.int32),
                pltpu.SMEM(class_effect.shape, F32),
                vmem((depth, width), BF16),
                vmem((width, depth), BF16),
                vmem((width, depth), BF16),
                vmem((depth, width), BF16),
                vmem((width, rows), BF16),
                vmem((n, rows, rows), BF16),
                vmem((width, rows), BF16),
                vmem((n, rows, rows), BF16),
                *buffers(2, width),
                *buffers(4, half),
                dma((3,)), dma((2,)), dma((2,)),
                dma((n,)), dma((n,)), dma((n,)), dma((n,)),
                *semaphores(2),
                *semaphores(4),
            ],
            compiler_params=pltpu.CompilerParams(
                collective_id=0, has_side_effects=True, vmem_limit_bytes=24 * 1024 * 1024
            ),
        )(dosage, trait_class.reshape(1, depth), class_effect)

    in_specs = (P("smp", "var"), P("smp"), P())
    out_specs = P(("var", "smp"), None)
    return jax.shard_map(shards, mesh=mesh, in_specs=in_specs, out_specs=out_specs, check_vma=False)
```

time: 186 us -> 46.7 us (0.25)
  waiting for transfers between devices: 151 us -> 0 us
  Pallas kernels: 0 us -> 43 us
  between operations: 14.1 us -> 0.01 us
  matrix products: 8.37 us -> 0 us
  other arithmetic: 5.05 us -> 0 us
  starting transfers between devices: 2.84 us -> 0 us
    reduce_scatter x2 -> x0, waiting for transfers between devices: 120 us -> none  [the longest x1 62.6 us: shards(): lax.psum_scatter(fourth, 'smp', scatter_dimension=0, tiled=True)]
    pallas_call x0 -> x1, Pallas kernels: none -> 43 us  [shards(): pl.pallas_call(functools.partial(kernel, nv, n), out_shape=jax.ShapeDtype...]
    ppermute x2 -> x0, waiting for transfers between devices: 31.7 us -> none  [from_behind(): return lax.ppermute(value, axis, pairs)]
    dot_general x2 -> x0, matrix products: 8.37 us -> none  [the longest x1 4.78 us: shards(): lax.dot_general(squared, right_sq, contract, preferred_element_type=jnp.f...]
    ppermute x2 -> x0, starting transfers between devices: 2.8 us -> none  [from_behind(): return lax.ppermute(value, axis, pairs)]
    div x1 -> x0, other arithmetic: 2.36 us -> none  [shards(): return cross / jnp.sqrt(fourth + 1e-05)]
    reduce_sum x2 -> x0, other arithmetic: 2.03 us -> none  [the longest x1 1.26 us: shards(): centred = class_effect - jnp.mean(class_effect)]
  transfers between devices with their start and end apart: 4 -> 0, of which waited for: 4 -> 0; matrix products, arithmetic and copies ran while one was open for 5% -> 0% of each run, Pallas kernels for 0% -> 0%
where the time goes in v3:
time: 46.7 us; the launch traced here: 46.5 us
  Pallas kernels  43 us (92%)
  local copies, waits for them, and re-layouts  3.45 us (7%)
    pallas_call x1, Pallas kernels, shards(): pl.pallas_call(functools.partial(kernel, nv, n), out_shape=jax.ShapeDtype...  43 us
    unnamed x7, local copies, waits for them, and re-layouts  3.45 us

profile of v3, /device:TPU:0, one launch (start us, length us, event | category | flops | bytes accessed | tf_op | source)
XLA Modules:
  0.0 46.5 jit_solution(13062815408123838914)
XLA Ops:
  0.0 0.0 copy-start.2
  0.0 0.7 %copy-done.2 = f32[16]{0:T(128)S(1)} copy-done((f32[16]{0:T(128)S(1)}, f32[16]{0:T(128)}, u32[]{:S(2)}) %copy-start.2) | copy-done | bytes 88
  0.7 0.0 copy-start
  0.7 1.2 %copy-done = bf16[1024,512]{1,0:T(8,128)(2,1)S(1)} copy-done((bf16[1024,512]{1,0:T(8,128)(2,1)S(1)}, bf16[1024,512]{1,0:T(8,128)(2,1)}, u32[]{:S(2)}) %copy-start) | copy-done | bytes 1048600
  1.9 0.0 copy-start.1
  1.9 0.7 %copy-done.1 = s32[1024]{0:T(1024)S(1)} copy-done((s32[1024]{0:T(1024)S(1)}, s32[1024]{0:T(1024)}, u32[]{:S(2)}) %copy-start.1) | copy-done | bytes 4120
  2.6 43.0 %shard_map.37 = f32[128,1536]{1,0:T(8,128)S(1)} custom-call(bf16[1024,512]{1,0:T(8,128)(2,1)S(1)} %copy-done, s32[1,1024]{1,0:T(1,128)S(1)} %bitcast.1, f32[16]{0:T(128)S(1)} %copy-done.2), custom_call_target="tpu_custom_call" | custom-call | tf_op jit(solution)/shard_map/pallas_call | solution.py:319
  45.6 0.9 %copy.5 = f32[128,1536]{1,0:T(8,128)} copy(f32[128,1536]{1,0:T(8,128)S(1)} %shard_map.37) | data formatting | bytes 1572864
Async XLA Ops:
  0.0 0.7 %copy-start.2 = (f32[16]{0:T(128)S(1)}, f32[16]{0:T(128)}, u32[]{:S(2)}) copy-start(f32[16]{0:T(128)} %effect_hbm.1) | copy-start | bytes 196
  0.7 1.2 %copy-start = (bf16[1024,512]{1,0:T(8,128)(2,1)S(1)}, bf16[1024,512]{1,0:T(8,128)(2,1)}, u32[]{:S(2)}) copy-start(bf16[1024,512]{1,0:T(8,128)(2,1)} %dosage_ref.1) | copy-start | bytes 3145732
  1.9 0.7 %copy-start.1 = (s32[1024]{0:T(1024)S(1)}, s32[1024]{0:T(1024)}, u32[]{:S(2)}) copy-start(s32[1024]{0:T(1024)} %param.4) | copy-start | bytes 12292

commit v4 on v3

--- a/solution.py
+++ b/solution.py
@@ -44,7 +44,6 @@
         pl.semaphore_signal(barrier, inc=1, device_id=(v, lax.rem(s + step, n)), device_id_type=MESH)
     for load in loads:
         load.wait()
-    pl.semaphore_wait(barrier, 3 * n - 1)
 
     def cols(h):
         return slice(h * half, (h + 1) * half)
@@ -55,9 +54,6 @@
             send_sem=d_send.at[h], recv_sem=d_recv.at[h],
             device_id=(prv, s), device_id_type=MESH,
         )
-
-    for h in range(2):
-        shift(h).start()
 
     classes = effect_ref.shape[0]
     mean = effect_ref[0]
@@ -152,6 +148,8 @@
             got = jnp.dot(left[...], right, preferred_element_type=F32)
             self.part[u] = got
             self.wire[u] = got.astype(BF16)
+
+        def send_relays(self, u):
             for k in range(1, pairs):
                 @pl.when(outer(k))
                 def _():
@@ -225,20 +223,44 @@
         return (values * values).astype(BF16)
 
     own.product(0, wt, d_ref[...])
+    pl.semaphore_wait(barrier, 3 * n - 1)
+    for h in range(2):
+        shift(h).start()
+    own.send_relays(0)
     sq[...] = squares(d_ref[...])
     own.product(1, qt, sq[...])
+    own.send_relays(1)
+    late = outer(1) if pairs > 1 else jnp.logical_and(odd == 0, odd == 1)
+
+    @pl.when(jnp.logical_not(late))
+    def _():
+        for u in range(2):
+            own.send_direct(u)
+
     for h in range(2):
         shift(h).wait_recv()
         follow.product(2 * h, wt, after[:, cols(h)])
+        follow.send_relays(2 * h)
         sq[:, cols(h)] = squares(after[:, cols(h)])
         follow.product(2 * h + 1, qt, sq[:, cols(h)])
+        follow.send_relays(2 * h + 1)
+
+        @pl.when(jnp.logical_not(late))
+        def _():
+            for u in range(2 * h, 2 * h + 2):
+                follow.send_direct(u)
+
         if h == 0:
             for u in range(2):
                 own.send_sums(u)
-    for u in range(4):
-        follow.send_direct(u)
-    for u in range(2):
-        own.send_direct(u)
+
+    @pl.when(late)
+    def _():
+        for u in range(4):
+            follow.send_direct(u)
+        for u in range(2):
+            own.send_direct(u)
+
     for u in range(4):
         follow.send_sums(u)
 
@@ -343,7 +365,7 @@
             compiler_params=pltpu.CompilerParams(
                 collective_id=0, has_side_effects=True, vmem_limit_bytes=24 * 1024 * 1024
             ),
-        )(dosage, trait_class.reshape(1, depth), class_effect)
+        )(*(pltpu.with_memory_space_constraint(x, pltpu.HBM) for x in (dosage, trait_class.reshape(1, depth), class_effect)))
 
     in_specs = (P("smp", "var"), P("smp"), P())
     out_specs = P(("var", "smp"), None)

time: 46.7 us -> 41.5 us (0.89)
  local copies, waits for them, and re-layouts: 3.45 us -> 0.88 us
  Pallas kernels: 43 us -> 40.5 us
    unnamed x7 -> x1, local copies, waits for them, and re-layouts: 3.45 us -> 0.88 us
    pallas_call x1, Pallas kernels: 43 us -> 40.5 us  [shards(): pl.pallas_call(functools.partial(kernel, nv, n), out_shape=jax.ShapeDtype...]
where the time goes in v4:
time: 41.5 us; the launch traced here: 41.4 us
  Pallas kernels  40.5 us (98%)
  local copies, waits for them, and re-layouts  0.88 us (2%)
    pallas_call x1, Pallas kernels, shards(): pl.pallas_call(functools.partial(kernel, nv, n), out_shape=jax.ShapeDtype...  40.5 us
    unnamed x1, local copies, waits for them, and re-layouts  0.88 us

profile of v4, /device:TPU:0, one launch (start us, length us, event | category | flops | bytes accessed | tf_op | source)
XLA Modules:
  0.0 41.4 jit_solution(11434549607981247659)
XLA Ops:
  0.0 40.5 %shard_map.37 = f32[128,1536]{1,0:T(8,128)S(1)} custom-call(bf16[1024,512]{1,0:T(8,128)(2,1)} %dosage_ref.1, s32[1,1024]{1,0:T(1,128)} %bitcast.1, f32[16]{0:T(128)} %effect_hbm.1), custom_call_target="tpu_custom_call" | custom-call | tf_op jit(solution)/shard_map/pallas_call | solution.py:341
  40.5 0.9 %copy.5 = f32[128,1536]{1,0:T(8,128)} copy(f32[128,1536]{1,0:T(8,128)S(1)} %shard_map.37) | data formatting | bytes 1572864

commit v5 on v4

--- a/solution.py
+++ b/solution.py
@@ -232,11 +232,8 @@
     own.send_relays(1)
     late = outer(1) if pairs > 1 else jnp.logical_and(odd == 0, odd == 1)
 
-    @pl.when(jnp.logical_not(late))
-    def _():
-        for u in range(2):
-            own.send_direct(u)
-
+    for u in range(2):
+        own.send_direct(u)
     for h in range(2):
         shift(h).wait_recv()
         follow.product(2 * h, wt, after[:, cols(h)])
@@ -258,8 +255,6 @@
     def _():
         for u in range(4):
             follow.send_direct(u)
-        for u in range(2):
-            own.send_direct(u)
 
     for u in range(4):
         follow.send_sums(u)

time: 41.5 us -> 40.9 us (0.986)
  Pallas kernels: 40.5 us -> 39.9 us
    pallas_call x1, Pallas kernels: 40.5 us -> 39.9 us  [shards(): pl.pallas_call(functools.partial(kernel, nv, n), out_shape=jax.ShapeDtype...]
where the time goes in v5:
time: 40.9 us; the launch traced here: 40.8 us
  Pallas kernels  39.9 us (98%)
  local copies, waits for them, and re-layouts  0.88 us (2%)
    pallas_call x1, Pallas kernels, shards(): pl.pallas_call(functools.partial(kernel, nv, n), out_shape=jax.ShapeDtype...  39.9 us
    unnamed x1, local copies, waits for them, and re-layouts  0.88 us

profile of v5, /device:TPU:0, one launch (start us, length us, event | category | flops | bytes accessed | tf_op | source)
XLA Modules:
  0.0 40.8 jit_solution(15165334824258531270)
XLA Ops:
  0.0 39.9 %shard_map.37 = f32[128,1536]{1,0:T(8,128)S(1)} custom-call(bf16[1024,512]{1,0:T(8,128)(2,1)} %dosage_ref.1, s32[1,1024]{1,0:T(1,128)} %bitcast.1, f32[16]{0:T(128)} %effect_hbm.1), custom_call_target="tpu_custom_call" | custom-call | tf_op jit(solution)/shard_map/pallas_call | solution.py:336
  39.9 0.9 %copy.5 = f32[128,1536]{1,0:T(8,128)} copy(f32[128,1536]{1,0:T(8,128)S(1)} %shard_map.37) | data formatting | bytes 1572864
